TPU v7x, 256 devices: a whole 4x4x8 slice. The times are simulated.
256 devices in a mesh: gx: 16 (over z, core), gy: 16 (over y, x).
Axes of the slice: x: 4, y: 4, z: 8, core: 2. Of those that a mesh axis runs over, the one named last changes fastest.
Arguments:
- fine_state: float32 [9, 8, 256, 4096], P(None, None, 'gx', 'gy'), may hold values from -6 to 6
- coarse_column_state: float32 [3, 9, 12, 128, 2048], P(None, None, None, 'gx', 'gy'), may hold values from -6 to 6
- diffusivity: float32 [9], replicated, may hold values from 0.02 to 0.08
- rates: float32 [9, 9], replicated, may hold values from -0.4 to 0.4
- owner_offset: int32 [16, 16], replicated, may hold values from -1 to 1
Outputs:
- fine_new: float32 [9, 8, 256, 4096], P(None, None, 'gx', 'gy')
- coarse_new: float32 [3, 9, 12, 128, 2048], P(None, None, None, 'gx', 'gy')
Inputs may be any that keep to these rules, and one draw needn't show every extreme that they name: The coarse column over fine box (i, j) lies in slot 1 - owner_offset[i, j] of the block at gy index (j + owner_offset[i, j]) mod 16 in the same gx row; a block owns zero to three columns.
All inputs are finite; a program needn't handle non-finite values.
Results may differ from a plain program's by a relative error of at most 0.0001.
Values sent between devices are 32-bit elements; how exact they have to be, the bound alone decides.
No kernel may reach another device: no remote copies, remote signals or barrier semaphores. Data moves between devices by JAX's collectives and lax.ppermute only.
A program may use at most 128 MiB of HBM per device.

v0:
```python
import jax
import jax.numpy as jnp
from jax import lax
from jax.experimental import pallas as pl
from jax.experimental.pallas import tpu as pltpu
from jax.sharding import PartitionSpec as P


F32 = jnp.float32
BF16 = jnp.bfloat16
NF = 9
NZ = 8
NX = 16
NY = 256
LOW = 3
HIGH = 8
VMEM = pltpu.VMEM
SMEM = pltpu.SMEM


def call(kernel, outs, spaces, flops, limit=8, aliases=None, scratch=(), out_spaces=None):
    return pl.pallas_call(
        kernel,
        out_shape=[jax.ShapeDtypeStruct(s, F32) for s in outs],
        in_specs=[pl.BlockSpec(memory_space=s) for s in spaces],
        out_specs=[pl.BlockSpec(memory_space=s) for s in out_spaces or [VMEM] * len(outs)],
        scratch_shapes=list(scratch),
        input_output_aliases=aliases or {},
        compiler_params=pltpu.CompilerParams(vmem_limit_bytes=int(limit * (1 << 20))),
        cost_estimate=pl.CostEstimate(flops=flops, bytes_accessed=1 << 20, transcendentals=0),
    )


def spread_table():
    coarse = lax.broadcasted_iota(jnp.int32, (128, 256), 0)
    fine = lax.broadcasted_iota(jnp.int32, (128, 256), 1)
    return jnp.where(lax.shift_right_logical(fine, 1) == coarse, 1.0, 0.0).astype(BF16)


def gather_table():
    fine = lax.broadcasted_iota(jnp.int32, (256, 128), 0)
    coarse = lax.broadcasted_iota(jnp.int32, (256, 128), 1)
    return jnp.where(lax.shift_right_logical(fine, 1) == coarse, 1.0, 0.0).astype(BF16)


def table_dot(value, table):
    high = value.astype(BF16)
    low = (value - high.astype(F32)).astype(BF16)
    return jnp.dot(high, table, preferred_element_type=F32) + jnp.dot(
        low, table, preferred_element_type=F32
    )


def reacted(tiles, f, scale, diagonal, rates):
    total = tiles[f] * (diagonal + scale * rates[f, f])
    for g in range(NF):
        if g != f:
            total = total + tiles[g] * (scale * rates[f, g])
    return total


def pack_columns(plane_of, side, fields=range(NF), packed=None):
    lane = lax.broadcasted_iota(jnp.int32, (NX, 128), 1)
    if packed is None:
        packed = jnp.zeros((NX, 128), F32)
    for f in fields:
        for z in range(NZ):
            at = z * 16 + f
            shift = at if side == 0 else (at - 127) % 128
            tile = plane_of(f, side, z)
            moved = pltpu.roll(tile, shift, 1) if shift else tile
            packed = jnp.where(lane == at, moved, packed)
    return packed


def split_plane(ref):
    return lambda f, h, z: ref[f, h, z * NX : (z + 1) * NX, :]


def whole_plane(ref):
    return lambda f, h, z: ref[f, z * NX : (z + 1) * NX, h * 128 : (h + 1) * 128]


def put_packs(packs, packed):
    for side in range(2):
        for t in range(2):
            packs[2 * side + t] = packed[side][8 * t : 8 * t + 8]


def kappa_lanes(kap):
    lane = lax.broadcasted_iota(jnp.int32, (NX, 128), 1) & 15
    out = jnp.zeros((NX, 128), F32)
    for f in range(NF):
        out = jnp.where(lane == f, 2.0 * kap[f], out)
    return out


def add_columns(ref, left, right):
    lane = lax.broadcasted_iota(jnp.int32, (NX, 128), 1)
    for z in range(NZ):
        rows = slice(z * NX, (z + 1) * NX)
        for f in range(NF):
            at = z * 16 + f
            moved = pltpu.roll(left, 128 - at, 1) if at else left
            ref[f, 0, rows, :] = ref[f, 0, rows, :] + jnp.where(lane == 0, moved, 0.0)
            shift = 127 - at
            moved = pltpu.roll(right, shift, 1) if shift else right
            ref[f, 1, rows, :] = ref[f, 1, rows, :] + jnp.where(lane == 127, moved, 0.0)


def row_of(ref, f, half, row):
    return ref[f, half, pl.ds(row, NZ, stride=NX), :]


def set_row(ref, f, half, row, value):
    ref[f, half, pl.ds(row, NZ, stride=NX), :] = value


def plane_at(z):
    start = z * NX
    return pl.ds(start if isinstance(z, int) else pl.multiple_of(start, NX), NX)


def substep(src, dst, mixed, k2, copy=None):
    lane = lax.broadcasted_iota(jnp.int32, (NX, 128), 1)

    def tile(f, h, z):
        if copy is None:
            return src[f, h, plane_at(z), :]
        return src[f, plane_at(z), h * 128 : (h + 1) * 128]

    def body(z, others):
        halves = [[tile(g, h, z) for g in range(NF)] for h in range(2)]
        for f in range(NF):
            a, b = halves[0][f], halves[1][f]
            a_up, b_up = pltpu.roll(a, 1, 1), pltpu.roll(b, 1, 1)
            a_down, b_down = pltpu.roll(a, 127, 1), pltpu.roll(b, 127, 1)
            sides = (
                jnp.where(lane == 0, b_up, a_up) + jnp.where(lane == 127, b_down, a_down),
                jnp.where(lane == 0, a_up, b_up) + jnp.where(lane == 127, a_down, b_down),
            )
            for h in range(2):
                v = halves[h][f]
                if copy is not None:
                    copy[f, h, plane_at(z), :] = v
                near = pltpu.roll(v, 1, 0) + pltpu.roll(v, NX - 1, 0) + sides[h]
                for other in others:
                    near = near + tile(f, h, other)
                dst[f, h, plane_at(z), :] = mixed(halves[h], f) + k2(f) * near

    body(0, (1,))

    def step(z, carry):
        body(z, (z - 1, z + 1))
        return carry

    lax.fori_loop(1, NZ - 1, step, 0)
    body(NZ - 1, (NZ - 2,))


def add_ghost(dst, z, tiles, kap):
    wide = table_dot(jnp.concatenate(tiles, axis=0), spread_table())
    for f in range(NF):
        for h in range(2):
            part = (2.0 * kap[f]) * wide[f * 8 : f * 8 + 8, h * 128 : (h + 1) * 128]
            for x in range(2):
                rows = pl.ds(z * NX + x, 8, stride=2)
                dst[f, h, rows, :] = dst[f, h, rows, :] + part


def is_even(axis):
    return (lax.axis_index(axis) & 1) == 0


def pick(flag, one, other):
    return jnp.where(flag, one, other)


def prep_kernel(c, u_in, u, odd, even, own, packs, sems):
    even_y = is_even("gy")
    fine = [
        pltpu.make_async_copy(u_in.at[3 * n : 3 * n + 3], u.at[3 * n : 3 * n + 3], sems.at[n])
        for n in range(3)
    ]
    copies = []
    for n, (slot, dst) in enumerate(((pick(even_y, 0, 2), odd), (pick(even_y, 2, 0), even), (1, own))):
        for side, k in ((0, LOW), (1, HIGH)):
            copies.append(
                pltpu.make_async_copy(
                    c.at[slot, :, k], dst.at[pl.ds(side * NF, NF)], sems.at[3 + 2 * n + side]
                )
            )
    for copy in fine + copies:
        copy.start()
    packed = [None, None]
    for n, copy in enumerate(fine):
        copy.wait()
        packed = [
            pack_columns(whole_plane(u), side, range(3 * n, 3 * n + 3), packed[side])
            for side in range(2)
        ]
    put_packs(packs, packed)
    for t in range(2):
        left, right = (packed[side][8 * t : 8 * t + 8] for side in range(2))
        odd[18 + t] = pick(even_y, left, right)
        even[18 + t] = pick(even_y, right, left)
    for copy in copies:
        copy.wait()


def pair_rows(ref, f, half, z):
    return (
        ref[f, half, pl.ds(z * NX, 8, stride=2), :]
        + ref[f, half, pl.ds(z * NX + 1, 8, stride=2), :]
    )


def tall(tile):
    return jnp.concatenate([tile, tile], axis=0)


class Shared:
    count = 95

    def __init__(self, ref):
        self.ref = ref

    def __getitem__(self, f):
        return self.ref[81 + f]

    def lanes(self):
        return self.ref[90]

    def flag(self, n):
        return self.ref[91 + n] > 0.5

    def mixed(self, tiles, f):
        total = tiles[0] * self.ref[f * NF]
        for g in range(1, NF):
            total = total + tiles[g] * self.ref[f * NF + g]
        return total

    def mixed_tall(self, tiles, f):
        total = tiles[0] * tall(self.ref[f * NF])
        for g in range(1, NF):
            total = total + tiles[g] * tall(self.ref[f * NF + g])
        return total


def fill_shared(shared, owner, kap, rates):
    for f in range(NF):
        for g in range(NF):
            value = 0.5 * rates[f, g]
            if f == g:
                value = value + (1.0 - 12.0 * kap[f])
            shared[f * NF + g] = jnp.full((8, 128), value, F32)
        shared[81 + f] = jnp.full((8, 128), kap[f], F32)
    shared[90] = kappa_lanes(kap)[0:8]
    mine = owner[lax.axis_index("gx"), lax.axis_index("gy")]
    left, _, right = used_flags(owner)
    flags = (mine == 0, mine == pick(is_even("gy"), -1, 1), left, right)
    for n, flag in enumerate(flags):
        shared[91 + n] = jnp.full((8, 128), jnp.where(flag, 1.0, 0.0), F32)


def inner1_kernel(
    u_in, c, kap, rates, owner, w, u, packs, sums, odd, even, own, shared, pairs
):
    fill_shared(shared, owner, kap, rates)
    substep(
        u_in,
        w,
        lambda tiles, f: reacted(tiles, f, 0.5, 1.0 - 12.0 * kap[f], rates),
        lambda f: 2.0 * kap[f],
        u,
    )
    for f in range(NF):
        k2 = 2.0 * kap[f]
        for h in range(2):
            set_row(w, f, h, 0, row_of(w, f, h, 0) - k2 * row_of(u, f, h, NX - 1))
            set_row(w, f, h, NX - 1, row_of(w, f, h, NX - 1) - k2 * row_of(u, f, h, 0))
    put_packs(packs, [pack_columns(split_plane(w), side) for side in range(2)])
    for side, z in ((0, 0), (1, NZ - 1)):
        for f in range(NF):
            for h in range(2):
                pairs[side * NF + f, :, h * 128 : (h + 1) * 128] = pair_rows(u, f, h, z) + pair_rows(
                    w, f, h, z
                )
    coarse = table_dot(pairs[...].reshape(18 * 8, NY), gather_table())
    for t in range(18):
        sums[t] = 0.25 * coarse[t * 8 : t * 8 + 8]
    even_y = is_even("gy")
    for slot, dst in ((pick(even_y, 0, 2), odd), (1, own), (pick(even_y, 2, 0), even)):
        for side, k in ((0, LOW), (1, HIGH)):
            tiles = [c[slot, g, k] for g in range(NF)]
            for f in range(NF):
                kf = kap[f]
                near = c[slot, f, k - 1] + c[slot, f, k + 1]
                dst[side * NF + f] = (
                    reacted(tiles, f, 0.5, 1.0 - kf, rates) + (0.5 * kf) * near
                )


def chosen(shared, odd, even, own, rims):
    at_own = shared.flag(0)
    at_odd = shared.flag(1)
    for t in range(18):
        rims[t] = jnp.where(at_own, own[t], jnp.where(at_odd, odd[t], even[t]))


def stacked(ref, at):
    return jnp.concatenate([ref[at], ref[at + 1]], axis=0)


def refined(tiles):
    return table_dot(jnp.concatenate(tiles, axis=0), spread_table())


def edges_kernel(
    u, w, odd_in, even_in, own, packs, packs_w, sums_w, y_odd_in, y_even_in, shared,
    y_odd, y_even, x_odd, x_even, rims, packs1, columns, sums, ghost,
):
    even_y = is_even("gy")
    even_x = is_even("gx")
    kap = Shared(shared)
    chosen(kap, odd_in, even_in, own, rims)
    k_lanes = tall(kap.lanes())
    odd, even = stacked(odd_in, 18), stacked(even_in, 18)
    from_left = pick(even_y, odd, even)
    from_right = pick(even_y, even, odd)
    left = k_lanes * (from_left - stacked(packs, 2))
    right = k_lanes * (from_right - stacked(packs, 0))
    put_packs(columns, [left, right])
    lane = lax.broadcasted_iota(jnp.int32, (8, 128), 1)
    for side in range(2):
        packed = jnp.zeros((8, 128), F32)
        for f in range(NF):
            for at, tile in ((f, rims[f]), (112 + f, rims[NF + f])):
                shift = at if side == 0 else (at - 127) % 128
                moved = pltpu.roll(tile, shift, 1) if shift else tile
                packed = jnp.where(lane == at, moved, packed)
        packed = packed * k_lanes[0:8]
        ghost[side, pl.ds(0, 8, stride=2), :] = packed
        ghost[side, pl.ds(1, 8, stride=2), :] = packed
    new_left = stacked(packs_w, 0) + left + ghost[0]
    new_right = stacked(packs_w, 2) + right + ghost[1]
    put_packs(packs1, [new_left, new_right])
    for t in range(2):
        a, b = new_left[8 * t : 8 * t + 8], new_right[8 * t : 8 * t + 8]
        y_odd[18 + t] = pick(even_y, a, b)
        y_even[18 + t] = pick(even_y, b, a)
    totals = []
    for side, value in enumerate((left, right)):
        ghost[side] = value
        totals.append(
            0.25 * (ghost[side, pl.ds(0, 8, stride=2), :] + ghost[side, pl.ds(1, 8, stride=2), :])
        )
    for side in range(2):
        for f in range(NF):
            kf = kap[f]
            at = 112 * side + f
            a = pltpu.roll(totals[0], 128 - at, 1) if at else totals[0]
            b = pltpu.roll(totals[1], 127 - at, 1)
            t = side * NF + f
            flux = sums_w[t] + jnp.where(lane == 0, a, jnp.where(lane == 127, b, 0.0))
            flux = flux + (2.0 * kf - 1.0) * rims[t]
            value = (-kf if side == 0 else kf) * flux
            sums[t] = value
            y_odd[20 + t] = value
            y_even[20 + t] = value
    wide_low = refined([rims[f] for f in range(NF)])
    wide_high = refined([rims[NF + f] for f in range(NF)])
    layer = lax.broadcasted_iota(jnp.int32, (NZ, 128), 0)
    for f in range(NF):
        k2 = 2.0 * kap[f]
        for h in range(2):
            lanes = slice(h * 128, (h + 1) * 128)
            first = row_of(u, f, h, 0)
            last = row_of(u, f, h, NX - 1)
            values = []
            for row, at in ((0, f * 8), (NX - 1, f * 8 + 7)):
                more = jnp.where(
                    layer == 0,
                    wide_low[at : at + 1, lanes],
                    jnp.where(layer == NZ - 1, wide_high[at : at + 1, lanes], 0.0),
                )
                values.append(row_of(w, f, h, row) + k2 * more)
            x_odd[2 * f + h] = pick(even_x, first, last)
            x_odd[18 + 2 * f + h] = pick(even_x, values[0], values[1])
            x_even[2 * f + h] = pick(even_x, last, first)
            x_even[18 + 2 * f + h] = pick(even_x, values[1], values[0])
    facing = (from_left, from_right, stacked(packs, 0), stacked(packs, 2))
    for n, value in enumerate(facing):
        x_odd[36 + n] = pick(even_x, value[0:8], value[8:16])
        x_even[36 + n] = pick(even_x, value[8:16], value[0:8])


def inner2_kernel(w, rims, columns, shared, u1, new, averages, sums):
    kap = Shared(shared)
    add_ghost(u1, 0, [rims[f] for f in range(NF)], kap)
    add_ghost(u1, NZ - 1, [rims[NF + f] for f in range(NF)], kap)
    add_columns(u1, stacked(columns, 0), stacked(columns, 2))
    substep(u1, new, kap.mixed_tall, lambda f: tall(2.0 * kap[f]))
    for f in range(NF):
        for h in range(2):
            lanes = slice(h * 128, (h + 1) * 128)
            for c in range(4):
                sums[f * 4 + c, :, lanes] = pair_rows(new, f, h, 2 * c) + pair_rows(
                    new, f, h, 2 * c + 1
                )
    table = gather_table()
    for f in range(NF):
        coarse = table_dot(sums[f * 4 : f * 4 + 4].reshape(32, NY), table)
        for c in range(4):
            averages[f * 4 + c] = coarse[c * 8 : c * 8 + 8] * 0.125


def row_terms(u, u1, message, kap, first, deltas, mores):
    here = pick(first, 0, NX - 1)
    opposite = pick(first, NX - 1, 0)
    layer = lax.broadcasted_iota(jnp.int32, (NZ, 128), 0)
    lane = lax.broadcasted_iota(jnp.int32, (NZ, 128), 1)
    delta = [[2.0 * kap[g] * message[2 * g + h] for g in range(NF)] for h in range(2)]
    for f in range(NF):
        k = kap[f]
        k2 = 2.0 * k
        a, b = delta[0][f], delta[1][f]
        a_up, b_up = pltpu.roll(a, 1, 1), pltpu.roll(b, 1, 1)
        a_down, b_down = pltpu.roll(a, 127, 1), pltpu.roll(b, 127, 1)
        sides = (
            jnp.where(lane == 0, b_up, a_up) + jnp.where(lane == 127, b_down, a_down),
            jnp.where(lane == 0, a_up, b_up) + jnp.where(lane == 127, a_down, b_down),
        )
        for h in range(2):
            d = delta[h][f]
            near = sides[h] + jnp.where(layer == 0, 0.0, pltpu.roll(d, 1, 0))
            near = near + jnp.where(layer == NZ - 1, 0.0, pltpu.roll(d, NZ - 1, 0))
            halo = message[18 + 2 * f + h] + k2 * row_of(u, f, h, here)
            near = near + (halo - row_of(u1, f, h, opposite))
            more = kap.mixed(delta[h], f) + k2 * near
            deltas[2 * f + h] = k2 * d
            mores[2 * f + h] = more
    return delta


def payload_kernel(
    u, u1, averages, x_odd, x_even, y_odd, y_even, own_mid, packs1, shared,
    payload, mids, deltas, mores, columns, pairs, rows,
):
    even_y = is_even("gy")
    even_x = is_even("gx")
    kap = Shared(shared)
    chosen(kap, y_odd, y_even, own_mid, mids)
    row_odd = pick(even_x, 0, 7)
    row_even = pick(even_x, 7, 0)
    for n, (message, first) in enumerate(((x_odd, even_x), (x_even, jnp.logical_not(even_x)))):
        delta = row_terms(u, u1, message, kap, first, deltas.at[n], mores.at[n])
        for f in range(NF):
            for h in range(2):
                lanes = slice(h * 128, (h + 1) * 128)
                rows[n, f, :, lanes] = mores[n, 2 * f + h] + deltas[n, 2 * f + h]
                rows[2 + n, f, :, lanes] = delta[h][f]
    table = gather_table()
    coarse = table_dot(rows[...].reshape(4 * NF * NZ, NY), table).reshape(4, NF, NZ, 128)
    k_lanes = tall(kap.lanes())
    x_id = lax.broadcasted_iota(jnp.int32, (NX, 128), 0)

    def facing(tile):
        low = pltpu.roll(pick(even_x, x_odd[tile], x_even[tile]), 1, 0)
        high = pltpu.roll(pick(even_x, x_even[tile], x_odd[tile]), 7, 0)
        both = jnp.concatenate([low, high], axis=0)
        return k_lanes * jnp.where((x_id == 0) | (x_id == NX - 1), both, 0.0)

    odd, even = stacked(y_odd, 18), stacked(y_even, 18)
    left = pick(even_y, odd, even) - stacked(packs1, 2) + 2.0 * (facing(36) - facing(39))
    right = pick(even_y, even, odd) - stacked(packs1, 0) + 2.0 * (facing(37) - facing(38))
    left = k_lanes * left
    right = k_lanes * right
    put_packs(columns, [left, right])
    side_sums = []
    for n, value in enumerate((left, right)):
        pairs[n] = value
        total = pairs[n, pl.ds(0, 8, stride=2), :] + pairs[n, pl.ds(1, 8, stride=2), :]
        side_sums.append(0.125 * (total + pltpu.roll(total, 112, 1)))
    row_id = lax.broadcasted_iota(jnp.int32, (8, 128), 0)
    lane = lax.broadcasted_iota(jnp.int32, (8, 128), 1)
    at_odd = row_id == row_odd
    at_even = row_id == row_even
    for f in range(NF):
        kf = kap[f]
        halves = [0.125 * (coarse[n, f] + pltpu.roll(coarse[n, f], NZ - 1, 0)) for n in range(2)]
        for c in range(4):
            value = averages[f * 4 + c]
            if c == 0:
                value = value + kf * mids[f]
            if c == 3:
                value = value + kf * mids[NF + f]
            z = 2 * c
            value = value + jnp.where(
                at_odd, halves[0][z : z + 1], jnp.where(at_even, halves[1][z : z + 1], 0.0)
            )
            at = z * 16 + f
            a = pltpu.roll(side_sums[0], 128 - at, 1) if at else side_sums[0]
            b = pltpu.roll(side_sums[1], 127 - at, 1) if at != 127 else side_sums[1]
            value = value + jnp.where(lane == 0, a, jnp.where(lane == 127, b, 0.0))
            payload[f * 4 + c] = value
        for side, z in ((0, 0), (1, NZ - 1)):
            for n in range(2):
                r = (side * NF + f) * 2 + n
                payload[36 + r // 8, r % 8 : r % 8 + 1, :] = (
                    0.25 * kf[0:1] * coarse[2 + n, f, z : z + 1]
                )


def fixes(payload, side, f):
    even_x = is_even("gx")
    row_id = lax.broadcasted_iota(jnp.int32, (8, 128), 0)
    r = (side * NF + f) * 2
    odd, even = (payload[36 + r // 8, r % 8 + n : r % 8 + n + 1, :] for n in range(2))
    return jnp.where(
        row_id == pick(even_x, 0, 7), odd, jnp.where(row_id == pick(even_x, 7, 0), even, 0.0)
    )


def assemble(new, mids, deltas, mores, columns, kap):
    even_x = is_even("gx")
    add_ghost(new, 0, [mids[f] for f in range(NF)], kap)
    add_ghost(new, NZ - 1, [mids[NF + f] for f in range(NF)], kap)
    for n, first in enumerate((even_x, jnp.logical_not(even_x))):
        here = pick(first, 0, NX - 1)
        inner = pick(first, 1, NX - 2)
        for f in range(NF):
            for h in range(2):
                at = 2 * f + h
                set_row(new, f, h, here, row_of(new, f, h, here) + mores[n, at])
                set_row(new, f, h, inner, row_of(new, f, h, inner) + deltas[n, at])
    add_columns(new, stacked(columns, 0), stacked(columns, 2))


def used_flags(owner):
    row = lax.axis_index("gx")
    col = lax.axis_index("gy")
    size = lax.axis_size("gy")
    left = owner[row, lax.rem(col + size - 1, size)] == 1
    self_used = owner[row, col] == 0
    right = owner[row, lax.rem(col + 1, size)] == -1
    return left, self_used, right


def coarse_kernel(
    c, new_in, payload, sums, mids, deltas, mores, columns, owner, kap, rates,
    out, fine_out, base, new, full, sems,
):
    assemble(new, mids, deltas, mores, columns, kap)
    copies = [
        pltpu.make_async_copy(new.at[:, h], fine_out.at[:, :, h * 128 : (h + 1) * 128], sems.at[h])
        for h in range(2)
    ]
    for copy in copies:
        copy.start()
    for slot, used in enumerate(used_flags(owner)):
        for k in (0, 1, 2, 3, 8, 9, 10, 11):
            tiles = [c[slot, g, k] for g in range(NF)]
            for f in range(NF):
                kf = kap[f]
                near = None
                count = 0.0
                if k not in (0, HIGH):
                    near = c[slot, f, k - 1]
                    count += 1.0
                if k not in (LOW, 11):
                    above = c[slot, f, k + 1]
                    near = above if near is None else near + above
                    count += 1.0
                value = reacted(tiles, f, 1.0, 1.0 - count * kf, rates) + kf * near
                if k in (LOW, HIGH):
                    beyond = c[slot, f, k + 1 if k == LOW else k - 1]
                    value = value - (0.5 * kf) * (tiles[f] + value + kf * (beyond - tiles[f]))
                    if slot != 1:
                        value = jnp.where(used, value, tiles[f])
                        base[slot // 2, f, k - LOW] = value
                    if slot == 1 and k == LOW:
                        value = value - sums[f] + fixes(payload, 0, f)
                    if slot == 1 and k == HIGH:
                        value = value + sums[NF + f] + fixes(payload, 1, f)
                full[slot, f, k] = jnp.where(used, value, tiles[f])
        for f in range(NF):
            for k in range(4, 8):
                value = c[slot, f, k]
                if slot == 1:
                    value = jnp.where(used, payload[f * 4 + k - 4], value)
                else:
                    base[slot // 2, f, k - LOW] = value
                full[slot, f, k] = value
        copy = pltpu.make_async_copy(full.at[slot], out.at[slot], sems.at[2 + slot])
        copy.start()
        copies.append(copy)
    for copy in copies:
        copy.wait()


def finish_kernel(out_in, base, odd, even, y_odd, y_even, shared, out, fixed, sems):
    kap = Shared(shared)
    even_y = is_even("gy")
    copies = []
    for n, slot in enumerate((0, 2)):
        used = kap.flag(2 + n)
        at_odd = even_y if n == 0 else jnp.logical_not(even_y)
        for f in range(NF):
            values = [pick(at_odd, odd[f * 4 + k], even[f * 4 + k]) for k in range(4)]
            low = pick(at_odd, fixes(odd, 0, f) - y_odd[20 + f], fixes(even, 0, f) - y_even[20 + f])
            high = pick(
                at_odd,
                fixes(odd, 1, f) + y_odd[20 + NF + f],
                fixes(even, 1, f) + y_even[20 + NF + f],
            )
            values = [base[n, f, 0] + low] + values + [base[n, f, 5] + high]
            for k in range(6):
                fixed[n, f, k] = jnp.where(used, values[k], base[n, f, k])
        copy = pltpu.make_async_copy(fixed.at[n], out.at[slot, :, LOW : HIGH + 1], sems.at[n])
        copy.start()
        copies.append(copy)
    for copy in copies:
        copy.wait()


def swapped(value, axis, odd):
    size = lax.axis_size(axis)
    pairs = []
    for i in range(odd, size, 2):
        j = (i + 1) % size
        pairs += [(i, j), (j, i)]
    return lax.ppermute(value, axis, pairs)


def on_device(fine_state, coarse_column_state, diffusivity, rates, owner_offset):
    fine_shape = fine_state.shape
    u_in = fine_state.reshape(NF, NZ * NX, NY)
    c = coarse_column_state
    split = (NF, 2, NZ * NX, 128)
    two = (2, 18, 8, 128)
    dma = pltpu.SemaphoreType.DMA

    def tiles(n):
        return (n, 8, 128)

    u, odd, even, own, packs = call(
        prep_kernel,
        [u_in.shape, tiles(20), tiles(20), tiles(18), tiles(4)],
        [pltpu.HBM, pltpu.HBM],
        1 << 20,
        limit=52,
        scratch=[dma((9,))],
    )(c, u_in)
    odd = swapped(odd, "gy", 1)
    even = swapped(even, "gy", 0)
    w, u, packs_w, sums_w, y_odd, y_even, own_mid, shared = call(
        inner1_kernel,
        [split, split] + [tiles(n) for n in (4, 18, 38, 38, 18, Shared.count)],
        [VMEM] * 2 + [SMEM] * 3,
        1 << 27,
        scratch=[pltpu.VMEM((18, 8, NY), F32)],
    )(u, c, diffusivity, rates, owner_offset)
    y_odd, y_even, x_odd, x_even, old, packs1, columns, sums = call(
        edges_kernel,
        [tiles(n) for n in (38, 38, 40, 40, 18, 4, 4, 18)],
        [VMEM] * 11,
        1 << 26,
        aliases={8: 0, 9: 1},
        scratch=[pltpu.VMEM((2, NX, 128), F32)],
    )(u, w, odd, even, own, packs, packs_w, sums_w, y_odd, y_even, shared)
    y_odd = swapped(y_odd, "gy", 1)
    x_odd = swapped(x_odd, "gx", 1)
    y_even = swapped(y_even, "gy", 0)
    x_even = swapped(x_even, "gx", 0)
    u1, new, averages = call(
        inner2_kernel,
        [split, split, tiles(36)],
        [VMEM] * 4,
        1 << 27,
        aliases={0: 0},
        scratch=[pltpu.VMEM((36, 8, NY), F32)],
    )(w, old, columns, shared)
    payload, mids, deltas, mores, columns = call(
        payload_kernel,
        [tiles(41), tiles(18), two, two, tiles(4)],
        [VMEM] * 10,
        1 << 26,
        scratch=[pltpu.VMEM((2, NX, 128), F32), pltpu.VMEM((4, NF, NZ, NY), F32)],
    )(
        u, u1, averages, x_odd, x_even, y_odd, y_even, own_mid, packs1, shared,
    )
    odd = swapped(payload, "gy", 1)
    even = swapped(payload, "gy", 0)
    out, fine_new, base, _ = call(
        coarse_kernel,
        [c.shape, u_in.shape, (2, NF, 6, 8, 128), split],
        [VMEM] * 8 + [SMEM] * 3,
        1 << 26,
        aliases={1: 3},
        scratch=[pltpu.VMEM(c.shape, F32), dma((5,))],
        out_spaces=[pltpu.HBM, pltpu.HBM, VMEM, VMEM],
    )(c, new, payload, sums, mids, deltas, mores, columns, owner_offset, diffusivity, rates)
    (coarse_new,) = call(
        finish_kernel,
        [c.shape],
        [pltpu.HBM] + [VMEM] * 6,
        1 << 20,
        aliases={0: 0},
        scratch=[pltpu.VMEM((2, NF, 6, 8, 128), F32), dma((2,))],
        out_spaces=[pltpu.HBM],
    )(out, base, odd, even, y_odd, y_even, shared)
    return fine_new.reshape(fine_shape), coarse_new


def solution(mesh):
    in_specs = (P(None, None, "gx", "gy"), P(None, None, None, "gx", "gy"), P(), P(), P())
    out_specs = (P(None, None, "gx", "gy"), P(None, None, None, "gx", "gy"))
    return jax.shard_map(
        on_device, mesh=mesh, in_specs=in_specs, out_specs=out_specs, check_vma=False
    )
```

profile of v0, /device:TPU:1, one launch (start us, length us, event | category | flops | bytes accessed | tf_op | source)
XLA Modules:
  0.0 36.5 jit_solution(4546032999621644976)
XLA Ops:
  0.7 1.7 %shard_map.68 = (f32[9,128,256]{2,1,0:T(8,128)S(1)}, f32[20,8,128]{2,1,0:T(8,128)S(1)}, f32[20,8,128]{2,1,0:T(8,128)S(1)}, f32[18,8,128]{2,1,0:T(8,128)S(1)}, f32[4,8,128]{2,1,0:T(8,128)S(1)}) custom-call(f32[3,9,12,8,128]{4,3,2,1,0:T(8,128)} %c.5, f32[9,128,256]{2,1,0:T(8,128)} %bitcast.2), custom_call_target="tpu_custom_call" | custom-call | flops 1048576 | bytes 1048576 | tf_op jit(solution)/shard_map/pallas_call | solution.py:647
  2.4 5.8 %collective-permute-start = (f32[20,8,128]{2,1,0:T(8,128)S(1)}, f32[20,8,128]{2,1,0:T(8,128)S(1)}, u32[]{:S(2)}, u32[]{:S(2)}) collective-permute-start(f32[20,8,128]{2,1,0:T(8,128)S(1)} %get-tuple-element.37), channel_id=1, source_target_pairs={{1,2},{2,1},{3,4},{4,3},{5,6},{6,5},{7,8},{8,7},{9,10},{10,9},{11,... | collective-permute-start | bytes 245768 | tf_op jit(solution)/shard_map/ppermute | solution.py:633
  8.2 0.0 collective-permute-start.1
  8.2 0.0 copy-done.2
  8.2 2.9 %shard_map.69 = (f32[9,2,128,128]{3,2,1,0:T(8,128)S(1)}, f32[9,2,128,128]{3,2,1,0:T(8,128)S(1)}, f32[4,8,128]{2,1,0:T(8,128)S(1)}, f32[18,8,128]{2,1,0:T(8,128)S...) custom-call(f32[9,128,256]{2,1,0:T(8,128)S(1)} %get-tuple-element.34, ...), custom_call_target="tpu_custom_call" | custom-call | flops 134217728 | bytes 1048576 | tf_op jit(solution)/shard_map/pallas_call | solution.py:657
  11.1 0.0 collective-permute-done.odd_in
  11.1 0.7 %collective-permute-done.1.even_in = f32[20,8,128]{2,1,0:T(8,128)S(1)} collective-permute-done((f32[20,8,128]{2,1,0:T(8,128)S(1)}, f32[20,8,128]{2,1,0:T(8,128)S(1)}, u32[]{:S(2)}, u32[]{:S(2)}) %collective-permute-start.1) | collective-permute-done | bytes 81952 | tf_op jit(solution)/shard_map/ppermute | solution.py:633
  11.8 0.3 shard_map.70
  12.1 3.4 %collective-permute-start.2 = (f32[40,8,128]{2,1,0:T(8,128)S(1)}, f32[40,8,128]{2,1,0:T(8,128)S(1)}, u32[]{:S(2)}, u32[]{:S(2)}) collective-permute-start(f32[40,8,128]{2,1,0:T(8,128)S(1)} %get-tuple-element.51), channel_id=1, source_target_pairs={{16,32},{32,16},{48,64},{64,48},{80,96},{96,80},{112,128},{128,112... | collective-permute-start | bytes 491528 | tf_op jit(solution)/shard_map/ppermute | solution.py:633
  15.5 2.3 %collective-permute-start.3 = (f32[40,8,128]{2,1,0:T(8,128)S(1)}, f32[40,8,128]{2,1,0:T(8,128)S(1)}, u32[]{:S(2)}, u32[]{:S(2)}) collective-permute-start(f32[40,8,128]{2,1,0:T(8,128)S(1)} %get-tuple-element.52), channel_id=1, source_target_pairs={{0,16},{16,0},{32,48},{48,32},{64,80},{80,64},{96,112},{112,96},{1... | collective-permute-start | bytes 491528 | tf_op jit(solution)/shard_map/ppermute | solution.py:633
  17.8 3.3 %collective-permute-start.4 = (f32[38,8,128]{2,1,0:T(8,128)S(1)}, f32[38,8,128]{2,1,0:T(8,128)S(1)}, u32[]{:S(2)}, u32[]{:S(2)}) collective-permute-start(f32[38,8,128]{2,1,0:T(8,128)S(1)} %get-tuple-element.53), channel_id=1, source_target_pairs={{1,2},{2,1},{3,4},{4,3},{5,6},{6,5},{7,8},{8,7},{9,10},{10,9},{11,... | collective-permute-start | bytes 466952 | tf_op jit(solution)/shard_map/ppermute | solution.py:633
  21.1 0.0 collective-permute-start.5
  21.1 2.0 %shard_map.71 = (f32[9,2,128,128]{3,2,1,0:T(8,128)S(1)}, f32[9,2,128,128]{3,2,1,0:T(8,128)S(1)}, f32[36,8,128]{2,1,0:T(8,128)S(1)}) custom-call(f32[9,2,128,128]{3,2,1,0:T(8,128)S(1)} %get-tuple-element.35.w, f32[18,8,128]{2,1,0:T(8,128)S(1)} %get-tuple-element.46.rims, f32[4,8,128]{2,1,0:T(8,128)S(1)} %get-tuple-element.47.columns, ...), custom_call_target="tpu_custom_call", output_to_operand_aliasing={{0}: (0, {})} | custom-call | flops 134217728 | bytes 1048576 | tf_op jit(solution)/shard_map/pallas_call | solution.py:676
  23.2 3.6 %collective-permute-done.4.y_odd = f32[38,8,128]{2,1,0:T(8,128)S(1)} collective-permute-done((f32[38,8,128]{2,1,0:T(8,128)S(1)}, f32[38,8,128]{2,1,0:T(8,128)S(1)}, u32[]{:S(2)}, u32[]{:S(2)}) %collective-permute-start.4) | collective-permute-done | bytes 155680 | tf_op jit(solution)/shard_map/ppermute | solution.py:633
  26.7 0.0 collective-permute-done.5.y_even
  26.7 0.0 collective-permute-done.2.x_odd
  26.7 0.0 collective-permute-done.3.x_even
  26.7 0.5 %shard_map.72 = (f32[41,8,128]{2,1,0:T(8,128)S(1)}, f32[18,8,128]{2,1,0:T(8,128)S(1)}, f32[2,18,8,128]{3,2,1,0:T(8,128)S(1)}, f32[2,18,8,128]{3,2,1,0:T(8,128)S(1)}, f32[4,8,128]{2,1,0:T(8,128)S(1)}) custom-call(f32[9,2,128,128]{3,2,1,0:T(8,128)S(1)} %get-tuple-element.36.u, f32[9,2,128,128]{3,2,1,0:T(8,128)S(1)} %get-tuple-element.49.u1, ...), custom_call_target="tpu_custom_call" | custom-call | flops 67108864 | bytes 1048576 | tf_op jit(solution)/shard_map/pallas_call | solution.py:684
  27.2 3.4 %collective-permute-start.6 = (f32[41,8,128]{2,1,0:T(8,128)S(1)}, f32[41,8,128]{2,1,0:T(8,128)S(1)}, u32[]{:S(2)}, u32[]{:S(2)}) collective-permute-start(f32[41,8,128]{2,1,0:T(8,128)S(1)} %get-tuple-element.57.payload), channel_id=1, source_target_pairs={{1,2},{2,1},{3,4},{4,3},{5,6},{6,5},{7,8},{8,7},{9,10},{10,9},{11,... | collective-permute-start | bytes 503816 | tf_op jit(solution)/shard_map/ppermute | solution.py:633
  30.6 0.0 collective-permute-start.7
  30.6 3.3 %shard_map.73 = (f32[3,9,12,8,128]{4,3,2,1,0:T(8,128)}, f32[9,128,256]{2,1,0:T(8,128)}, f32[2,9,6,8,128]{4,3,2,1,0:T(8,128)S(1)}, f32[9,2,128,128]{3,2,1,0:T(8,128)S(1)}) custom-call(f32[3,9,12,8,128]{4,3,2,1,0:T(8,128)S(1)} %copy-done, f32[9,2,128,128]{3,2,1,0:T(8,128)S(1)} %get-tuple-element.48.new_in, ...), custom_call_target="tpu_custom_call", output_to_operand_aliasing={{3}: (1, {})} | custom-call | flops 67108864 | bytes 1048576 | tf_op jit(solution)/shard_map/pallas_call | solution.py:695
  34.0 1.7 %collective-permute-done.6.odd = f32[41,8,128]{2,1,0:T(8,128)S(1)} collective-permute-done((f32[41,8,128]{2,1,0:T(8,128)S(1)}, f32[41,8,128]{2,1,0:T(8,128)S(1)}, u32[]{:S(2)}, u32[]{:S(2)}) %collective-permute-start.6) | collective-permute-done | bytes 167968 | tf_op jit(solution)/shard_map/ppermute | solution.py:633
  35.6 0.0 collective-permute-done.7.even
  35.6 0.8 %shard_map.74 = f32[3,9,12,8,128]{4,3,2,1,0:T(8,128)} custom-call(f32[3,9,12,8,128]{4,3,2,1,0:T(8,128)} %get-tuple-element.64.out_in, f32[2,9,6,8,128]{4,3,2,1,0:T(8,128)S(1)} %get-tuple-element.65.base, f32[41,8,128]{2,1,0:T(8,128)S(1)} %collective-permute-done.6.odd, ...), custom_call_target="tpu_custom_call", output_to_operand_aliasing={{}: (0, {})} | custom-call | flops 1048576 | bytes 1048576 | tf_op jit(solution)/shard_map/pallas_call | solution.py:704
  (7 shorter events, 0.0 us)
Async XLA Ops:
  0.6 7.6 %copy-start = (f32[3,9,12,8,128]{4,3,2,1,0:T(8,128)S(1)}, f32[3,9,12,8,128]{4,3,2,1,0:T(8,128)}, u32[]{:S(2)}) copy-start(f32[3,9,12,8,128]{4,3,2,1,0:T(8,128)} %c.5) | copy-start | bytes 3981316
  0.6 7.6 %copy-start.1 = (f32[9,9]{1,0:T(8,128)S(1)}, f32[9,9]{1,0:T(8,128)}, u32[]{:S(2)}) copy-start(f32[9,9]{1,0:T(8,128)} %rates.3) | copy-start | bytes 976
  0.7 7.6 %copy-start.2 = (s32[16,16]{1,0:T(8,128)S(1)}, s32[16,16]{1,0:T(8,128)}, u32[]{:S(2)}) copy-start(s32[16,16]{1,0:T(8,128)} %owner.3) | copy-start | bytes 3076
  0.7 7.6 %copy-start.3 = (f32[9]{0:T(128)S(1)}, f32[9]{0:T(128)}, u32[]{:S(2)}) copy-start(f32[9]{0:T(128)} %kap.3) | copy-start | bytes 112
  2.4 8.7 %collective-permute-start = (f32[20,8,128]{2,1,0:T(8,128)S(1)}, f32[20,8,128]{2,1,0:T(8,128)S(1)}, u32[]{:S(2)}, u32[]{:S(2)}) collective-permute-start(f32[20,8,128]{2,1,0:T(8,128)S(1)} %get-tuple-element.37), channel_id=1, source_target_pairs={{1,2},{2,1},{3,4},{4,3},{5,6},{6,5},{7,8},{8,7},{9,10},{10,9},{11,... | collective-permute-start | bytes 245768 | tf_op jit(solution)/shard_map/ppermute | solution.py:633
  8.2 3.6 %collective-permute-start.1 = (f32[20,8,128]{2,1,0:T(8,128)S(1)}, f32[20,8,128]{2,1,0:T(8,128)S(1)}, u32[]{:S(2)}, u32[]{:S(2)}) collective-permute-start(f32[20,8,128]{2,1,0:T(8,128)S(1)} %get-tuple-element.38), channel_id=1, source_target_pairs={{0,1},{1,0},{2,3},{3,2},{4,5},{5,4},{6,7},{7,6},{8,9},{9,8},{10,11... | collective-permute-start | bytes 245768 | tf_op jit(solution)/shard_map/ppermute | solution.py:633
  12.1 14.7 %collective-permute-start.2 = (f32[40,8,128]{2,1,0:T(8,128)S(1)}, f32[40,8,128]{2,1,0:T(8,128)S(1)}, u32[]{:S(2)}, u32[]{:S(2)}) collective-permute-start(f32[40,8,128]{2,1,0:T(8,128)S(1)} %get-tuple-element.51), channel_id=1, source_target_pairs={{16,32},{32,16},{48,64},{64,48},{80,96},{96,80},{112,128},{128,112... | collective-permute-start | bytes 491528 | tf_op jit(solution)/shard_map/ppermute | solution.py:633
  15.5 11.3 %collective-permute-start.3 = (f32[40,8,128]{2,1,0:T(8,128)S(1)}, f32[40,8,128]{2,1,0:T(8,128)S(1)}, u32[]{:S(2)}, u32[]{:S(2)}) collective-permute-start(f32[40,8,128]{2,1,0:T(8,128)S(1)} %get-tuple-element.52), channel_id=1, source_target_pairs={{0,16},{16,0},{32,48},{48,32},{64,80},{80,64},{96,112},{112,96},{1... | collective-permute-start | bytes 491528 | tf_op jit(solution)/shard_map/ppermute | solution.py:633
  17.8 8.9 %collective-permute-start.4 = (f32[38,8,128]{2,1,0:T(8,128)S(1)}, f32[38,8,128]{2,1,0:T(8,128)S(1)}, u32[]{:S(2)}, u32[]{:S(2)}) collective-permute-start(f32[38,8,128]{2,1,0:T(8,128)S(1)} %get-tuple-element.53), channel_id=1, source_target_pairs={{1,2},{2,1},{3,4},{4,3},{5,6},{6,5},{7,8},{8,7},{9,10},{10,9},{11,... | collective-permute-start | bytes 466952 | tf_op jit(solution)/shard_map/ppermute | solution.py:633
  21.1 5.6 %collective-permute-start.5 = (f32[38,8,128]{2,1,0:T(8,128)S(1)}, f32[38,8,128]{2,1,0:T(8,128)S(1)}, u32[]{:S(2)}, u32[]{:S(2)}) collective-permute-start(f32[38,8,128]{2,1,0:T(8,128)S(1)} %get-tuple-element.54), channel_id=1, source_target_pairs={{0,1},{1,0},{2,3},{3,2},{4,5},{5,4},{6,7},{7,6},{8,9},{9,8},{10,11... | collective-permute-start | bytes 466952 | tf_op jit(solution)/shard_map/ppermute | solution.py:633
  27.2 8.4 %collective-permute-start.6 = (f32[41,8,128]{2,1,0:T(8,128)S(1)}, f32[41,8,128]{2,1,0:T(8,128)S(1)}, u32[]{:S(2)}, u32[]{:S(2)}) collective-permute-start(f32[41,8,128]{2,1,0:T(8,128)S(1)} %get-tuple-element.57.payload), channel_id=1, source_target_pairs={{1,2},{2,1},{3,4},{4,3},{5,6},{6,5},{7,8},{8,7},{9,10},{10,9},{11,... | collective-permute-start | bytes 503816 | tf_op jit(solution)/shard_map/ppermute | solution.py:633
  30.6 5.0 %collective-permute-start.7 = (f32[41,8,128]{2,1,0:T(8,128)S(1)}, f32[41,8,128]{2,1,0:T(8,128)S(1)}, u32[]{:S(2)}, u32[]{:S(2)}) collective-permute-start(f32[41,8,128]{2,1,0:T(8,128)S(1)} %get-tuple-element.57.payload), channel_id=1, source_target_pairs={{0,1},{1,0},{2,3},{3,2},{4,5},{5,4},{6,7},{7,6},{8,9},{9,8},{10,11... | collective-permute-start | bytes 503816 | tf_op jit(solution)/shard_map/ppermute | solution.py:633
where the time goes:
time: 36.6 us; the launch traced here: 36.5 us
  starting transfers between devices  18.3 us (50%)
  Pallas kernels  11.5 us (31%)
  waiting for transfers between devices  5.9 us (16%)
  between operations  0.74 us (2%)
    ppermute x8, starting transfers between devices, swapped(): return lax.ppermute(value, axis, pairs)  18.3 us
    ppermute x8, waiting for transfers between devices, swapped(): return lax.ppermute(value, axis, pairs)  5.9 us
    pallas_call x1, Pallas kernels, on_device(): call(coarse_kernel, [c.shape, u_in.shape, (2, NF, 6, 8, 128), split], [VM...  3.3 us
    pallas_call x1, Pallas kernels, on_device(): call(inner1_kernel, [split, split] + [tiles(n) for n in (4, 18, 38, 38, 1...  2.87 us
    pallas_call x1, Pallas kernels, on_device(): call(inner2_kernel, [split, split, tiles(36)], [VMEM] * 4, 1 << 27, alias...  2.01 us
    pallas_call x1, Pallas kernels, on_device(): call(prep_kernel, [u_in.shape, tiles(20), tiles(20), tiles(18), tiles(4)]...  1.69 us
    pallas_call x1, Pallas kernels, on_device(): call(finish_kernel, [c.shape], [pltpu.HBM] + [VMEM] * 6, 1 << 20, aliases...  0.85 us
  transfers between devices with their start and end apart: 8, of which 3 were waited for; matrix products, arithmetic and copies ran while one was open for 0% of the time, Pallas kernels for 22%

commit v1 on v0

--- a/solution.py
+++ b/solution.py
@@ -389,10 +389,11 @@
             x_odd[18 + 2 * f + h] = pick(even_x, values[0], values[1])
             x_even[2 * f + h] = pick(even_x, last, first)
             x_even[18 + 2 * f + h] = pick(even_x, values[1], values[0])
-    facing = (from_left, from_right, stacked(packs, 0), stacked(packs, 2))
-    for n, value in enumerate(facing):
-        x_odd[36 + n] = pick(even_x, value[0:8], value[8:16])
-        x_even[36 + n] = pick(even_x, value[8:16], value[0:8])
+    row_id = lax.broadcasted_iota(jnp.int32, (8, 128), 0)
+    top = jnp.where(row_id == 0, left[0:1], right[0:1])
+    bottom = jnp.where(row_id == 0, left[NX - 1 : NX], right[NX - 1 : NX])
+    x_odd[36] = pick(even_x, top, bottom)
+    x_even[36] = pick(even_x, bottom, top)
 
 
 def inner2_kernel(w, rims, columns, shared, u1, new, averages, sums):
@@ -465,15 +466,16 @@
     k_lanes = tall(kap.lanes())
     x_id = lax.broadcasted_iota(jnp.int32, (NX, 128), 0)
 
-    def facing(tile):
-        low = pltpu.roll(pick(even_x, x_odd[tile], x_even[tile]), 1, 0)
-        high = pltpu.roll(pick(even_x, x_even[tile], x_odd[tile]), 7, 0)
-        both = jnp.concatenate([low, high], axis=0)
-        return k_lanes * jnp.where((x_id == 0) | (x_id == NX - 1), both, 0.0)
+    low = pick(even_x, x_odd[36], x_even[36])
+    high = pick(even_x, x_even[36], x_odd[36])
+
+    def corner(n):
+        at_high = jnp.where(x_id == NX - 1, high[n : n + 1], 0.0)
+        return 2.0 * jnp.where(x_id == 0, low[n : n + 1], at_high)
 
     odd, even = stacked(y_odd, 18), stacked(y_even, 18)
-    left = pick(even_y, odd, even) - stacked(packs1, 2) + 2.0 * (facing(36) - facing(39))
-    right = pick(even_y, even, odd) - stacked(packs1, 0) + 2.0 * (facing(37) - facing(38))
+    left = pick(even_y, odd, even) - stacked(packs1, 2) + corner(0)
+    right = pick(even_y, even, odd) - stacked(packs1, 0) + corner(1)
     left = k_lanes * left
     right = k_lanes * right
     put_packs(columns, [left, right])
@@ -663,7 +665,7 @@
     )(u, c, diffusivity, rates, owner_offset)
     y_odd, y_even, x_odd, x_even, old, packs1, columns, sums = call(
         edges_kernel,
-        [tiles(n) for n in (38, 38, 40, 40, 18, 4, 4, 18)],
+        [tiles(n) for n in (38, 38, 37, 37, 18, 4, 4, 18)],
         [VMEM] * 11,
         1 << 26,
         aliases={8: 0, 9: 1},

time: 36.6 us -> 33.1 us (0.904)
  waiting for transfers between devices: 5.9 us -> 4.15 us
  starting transfers between devices: 18.3 us -> 16.6 us
    ppermute x8, starting transfers between devices: 18.3 us -> 16.6 us  [swapped(): return lax.ppermute(value, axis, pairs)]
    ppermute x8, waiting for transfers between devices: 5.9 us -> 4.15 us  [swapped(): return lax.ppermute(value, axis, pairs)]
  transfers between devices with their start and end apart: 8 -> 8, of which waited for: 3 -> 2; matrix products, arithmetic and copies ran while one was open for 0% -> 0% of each run, Pallas kernels for 22% -> 25%
where the time goes in v1:
time: 33.1 us; the launch traced here: 33 us
  starting transfers between devices  16.6 us (50%)
  Pallas kernels  11.5 us (35%)
  waiting for transfers between devices  4.15 us (13%)
  between operations  0.77 us (2%)
    ppermute x8, starting transfers between devices, swapped(): return lax.ppermute(value, axis, pairs)  16.6 us
    ppermute x8, waiting for transfers between devices, swapped(): return lax.ppermute(value, axis, pairs)  4.15 us
    pallas_call x1, Pallas kernels, on_device(): call(coarse_kernel, [c.shape, u_in.shape, (2, NF, 6, 8, 128), split], [VM...  3.31 us
    pallas_call x1, Pallas kernels, on_device(): call(inner1_kernel, [split, split] + [tiles(n) for n in (4, 18, 38, 38, 1...  2.87 us
    pallas_call x1, Pallas kernels, on_device(): call(inner2_kernel, [split, split, tiles(36)], [VMEM] * 4, 1 << 27, alias...  2.02 us
    pallas_call x1, Pallas kernels, on_device(): call(prep_kernel, [u_in.shape, tiles(20), tiles(20), tiles(18), tiles(4)]...  1.69 us
    pallas_call x1, Pallas kernels, on_device(): call(finish_kernel, [c.shape], [pltpu.HBM] + [VMEM] * 6, 1 << 20, aliases...  0.85 us
  transfers between devices with their start and end apart: 8, of which 2 were waited for; matrix products, arithmetic and copies ran while one was open for 0% of the time, Pallas kernels for 25%

profile of v1, /device:TPU:1, one launch (start us, length us, event | category | flops | bytes accessed | tf_op | source)
XLA Modules:
  0.0 33.0 jit_solution(13358393643116700399)
XLA Ops:
  0.7 1.7 %shard_map.68 = (f32[9,128,256]{2,1,0:T(8,128)S(1)}, f32[20,8,128]{2,1,0:T(8,128)S(1)}, f32[20,8,128]{2,1,0:T(8,128)S(1)}, f32[18,8,128]{2,1,0:T(8,128)S(1)}, f32[4,8,128]{2,1,0:T(8,128)S(1)}) custom-call(f32[3,9,12,8,128]{4,3,2,1,0:T(8,128)} %c.5, f32[9,128,256]{2,1,0:T(8,128)} %bitcast.2), custom_call_target="tpu_custom_call" | custom-call | flops 1048576 | bytes 1048576 | tf_op jit(solution)/shard_map/pallas_call | solution.py:649
  2.4 5.8 %collective-permute-start = (f32[20,8,128]{2,1,0:T(8,128)S(1)}, f32[20,8,128]{2,1,0:T(8,128)S(1)}, u32[]{:S(2)}, u32[]{:S(2)}) collective-permute-start(f32[20,8,128]{2,1,0:T(8,128)S(1)} %get-tuple-element.37), channel_id=1, source_target_pairs={{1,2},{2,1},{3,4},{4,3},{5,6},{6,5},{7,8},{8,7},{9,10},{10,9},{11,... | collective-permute-start | bytes 245768 | tf_op jit(solution)/shard_map/ppermute | solution.py:635
  8.2 0.0 collective-permute-start.1
  8.2 0.0 copy-done.2
  8.2 2.9 %shard_map.69 = (f32[9,2,128,128]{3,2,1,0:T(8,128)S(1)}, f32[9,2,128,128]{3,2,1,0:T(8,128)S(1)}, f32[4,8,128]{2,1,0:T(8,128)S(1)}, f32[18,8,128]{2,1,0:T(8,128)S...) custom-call(f32[9,128,256]{2,1,0:T(8,128)S(1)} %get-tuple-element.34, ...), custom_call_target="tpu_custom_call" | custom-call | flops 134217728 | bytes 1048576 | tf_op jit(solution)/shard_map/pallas_call | solution.py:659
  11.1 0.0 collective-permute-done.odd_in
  11.1 0.7 %collective-permute-done.1.even_in = f32[20,8,128]{2,1,0:T(8,128)S(1)} collective-permute-done((f32[20,8,128]{2,1,0:T(8,128)S(1)}, f32[20,8,128]{2,1,0:T(8,128)S(1)}, u32[]{:S(2)}, u32[]{:S(2)}) %collective-permute-start.1) | collective-permute-done | bytes 81952 | tf_op jit(solution)/shard_map/ppermute | solution.py:635
  11.8 0.3 shard_map.70
  12.1 3.1 %collective-permute-start.4 = (f32[38,8,128]{2,1,0:T(8,128)S(1)}, f32[38,8,128]{2,1,0:T(8,128)S(1)}, u32[]{:S(2)}, u32[]{:S(2)}) collective-permute-start(f32[38,8,128]{2,1,0:T(8,128)S(1)} %get-tuple-element.53), channel_id=1, source_target_pairs={{1,2},{2,1},{3,4},{4,3},{5,6},{6,5},{7,8},{8,7},{9,10},{10,9},{11,... | collective-permute-start | bytes 466952 | tf_op jit(solution)/shard_map/ppermute | solution.py:635
  15.2 0.0 collective-permute-start.5
  15.2 3.6 %collective-permute-start.2 = (f32[37,8,128]{2,1,0:T(8,128)S(1)}, f32[37,8,128]{2,1,0:T(8,128)S(1)}, u32[]{:S(2)}, u32[]{:S(2)}) collective-permute-start(f32[37,8,128]{2,1,0:T(8,128)S(1)} %get-tuple-element.51), channel_id=1, source_target_pairs={{16,32},{32,16},{48,64},{64,48},{80,96},{96,80},{112,128},{128,112... | collective-permute-start | bytes 454664 | tf_op jit(solution)/shard_map/ppermute | solution.py:635
  18.8 2.3 %collective-permute-start.3 = (f32[37,8,128]{2,1,0:T(8,128)S(1)}, f32[37,8,128]{2,1,0:T(8,128)S(1)}, u32[]{:S(2)}, u32[]{:S(2)}) collective-permute-start(f32[37,8,128]{2,1,0:T(8,128)S(1)} %get-tuple-element.52), channel_id=1, source_target_pairs={{0,16},{16,0},{32,48},{48,32},{64,80},{80,64},{96,112},{112,96},{1... | collective-permute-start | bytes 454664 | tf_op jit(solution)/shard_map/ppermute | solution.py:635
  21.1 2.0 %shard_map.71 = (f32[9,2,128,128]{3,2,1,0:T(8,128)S(1)}, f32[9,2,128,128]{3,2,1,0:T(8,128)S(1)}, f32[36,8,128]{2,1,0:T(8,128)S(1)}) custom-call(f32[9,2,128,128]{3,2,1,0:T(8,128)S(1)} %get-tuple-element.35.w, f32[18,8,128]{2,1,0:T(8,128)S(1)} %get-tuple-element.46.rims, f32[4,8,128]{2,1,0:T(8,128)S(1)} %get-tuple-element.47.columns, ...), custom_call_target="tpu_custom_call", output_to_operand_aliasing={{0}: (0, {})} | custom-call | flops 134217728 | bytes 1048576 | tf_op jit(solution)/shard_map/pallas_call | solution.py:678
  23.2 0.0 collective-permute-done.2.x_odd
  23.2 0.0 collective-permute-done.3.x_even
  23.2 0.0 collective-permute-done.4.y_odd
  23.2 0.0 collective-permute-done.5.y_even
  23.2 0.5 %shard_map.72 = (f32[41,8,128]{2,1,0:T(8,128)S(1)}, f32[18,8,128]{2,1,0:T(8,128)S(1)}, f32[2,18,8,128]{3,2,1,0:T(8,128)S(1)}, f32[2,18,8,128]{3,2,1,0:T(8,128)S(1)}, f32[4,8,128]{2,1,0:T(8,128)S(1)}) custom-call(f32[9,2,128,128]{3,2,1,0:T(8,128)S(1)} %get-tuple-element.36.u, f32[9,2,128,128]{3,2,1,0:T(8,128)S(1)} %get-tuple-element.49.u1, ...), custom_call_target="tpu_custom_call" | custom-call | flops 67108864 | bytes 1048576 | tf_op jit(solution)/shard_map/pallas_call | solution.py:686
  23.7 1.5 %collective-permute-start.6 = (f32[41,8,128]{2,1,0:T(8,128)S(1)}, f32[41,8,128]{2,1,0:T(8,128)S(1)}, u32[]{:S(2)}, u32[]{:S(2)}) collective-permute-start(f32[41,8,128]{2,1,0:T(8,128)S(1)} %get-tuple-element.57.payload), channel_id=1, source_target_pairs={{1,2},{2,1},{3,4},{4,3},{5,6},{6,5},{7,8},{8,7},{9,10},{10,9},{11,... | collective-permute-start | bytes 503816 | tf_op jit(solution)/shard_map/ppermute | solution.py:635
  25.3 0.1 collective-permute-start.7
  25.4 3.3 %shard_map.73 = (f32[3,9,12,8,128]{4,3,2,1,0:T(8,128)}, f32[9,128,256]{2,1,0:T(8,128)}, f32[2,9,6,8,128]{4,3,2,1,0:T(8,128)S(1)}, f32[9,2,128,128]{3,2,1,0:T(8,128)S(1)}) custom-call(f32[3,9,12,8,128]{4,3,2,1,0:T(8,128)S(1)} %copy-done, f32[9,2,128,128]{3,2,1,0:T(8,128)S(1)} %get-tuple-element.48.new_in, ...), custom_call_target="tpu_custom_call", output_to_operand_aliasing={{3}: (1, {})} | custom-call | flops 67108864 | bytes 1048576 | tf_op jit(solution)/shard_map/pallas_call | solution.py:697
  28.7 3.5 %collective-permute-done.6.odd = f32[41,8,128]{2,1,0:T(8,128)S(1)} collective-permute-done((f32[41,8,128]{2,1,0:T(8,128)S(1)}, f32[41,8,128]{2,1,0:T(8,128)S(1)}, u32[]{:S(2)}, u32[]{:S(2)}) %collective-permute-start.6) | collective-permute-done | bytes 167968 | tf_op jit(solution)/shard_map/ppermute | solution.py:635
  32.2 0.0 collective-permute-done.7.even
  32.2 0.8 %shard_map.74 = f32[3,9,12,8,128]{4,3,2,1,0:T(8,128)} custom-call(f32[3,9,12,8,128]{4,3,2,1,0:T(8,128)} %get-tuple-element.64.out_in, f32[2,9,6,8,128]{4,3,2,1,0:T(8,128)S(1)} %get-tuple-element.65.base, f32[41,8,128]{2,1,0:T(8,128)S(1)} %collective-permute-done.6.odd, ...), custom_call_target="tpu_custom_call", output_to_operand_aliasing={{}: (0, {})} | custom-call | flops 1048576 | bytes 1048576 | tf_op jit(solution)/shard_map/pallas_call | solution.py:706
  (7 shorter events, 0.0 us)
Async XLA Ops:
  0.6 7.6 %copy-start = (f32[3,9,12,8,128]{4,3,2,1,0:T(8,128)S(1)}, f32[3,9,12,8,128]{4,3,2,1,0:T(8,128)}, u32[]{:S(2)}) copy-start(f32[3,9,12,8,128]{4,3,2,1,0:T(8,128)} %c.5) | copy-start | bytes 3981316
  0.6 7.6 %copy-start.1 = (f32[9,9]{1,0:T(8,128)S(1)}, f32[9,9]{1,0:T(8,128)}, u32[]{:S(2)}) copy-start(f32[9,9]{1,0:T(8,128)} %rates.3) | copy-start | bytes 976
  0.7 7.6 %copy-start.2 = (s32[16,16]{1,0:T(8,128)S(1)}, s32[16,16]{1,0:T(8,128)}, u32[]{:S(2)}) copy-start(s32[16,16]{1,0:T(8,128)} %owner.3) | copy-start | bytes 3076
  0.7 7.6 %copy-start.3 = (f32[9]{0:T(128)S(1)}, f32[9]{0:T(128)}, u32[]{:S(2)}) copy-start(f32[9]{0:T(128)} %kap.3) | copy-start | bytes 112
  2.4 8.7 %collective-permute-start = (f32[20,8,128]{2,1,0:T(8,128)S(1)}, f32[20,8,128]{2,1,0:T(8,128)S(1)}, u32[]{:S(2)}, u32[]{:S(2)}) collective-permute-start(f32[20,8,128]{2,1,0:T(8,128)S(1)} %get-tuple-element.37), channel_id=1, source_target_pairs={{1,2},{2,1},{3,4},{4,3},{5,6},{6,5},{7,8},{8,7},{9,10},{10,9},{11,... | collective-permute-start | bytes 245768 | tf_op jit(solution)/shard_map/ppermute | solution.py:635
  8.2 3.6 %collective-permute-start.1 = (f32[20,8,128]{2,1,0:T(8,128)S(1)}, f32[20,8,128]{2,1,0:T(8,128)S(1)}, u32[]{:S(2)}, u32[]{:S(2)}) collective-permute-start(f32[20,8,128]{2,1,0:T(8,128)S(1)} %get-tuple-element.38), channel_id=1, source_target_pairs={{0,1},{1,0},{2,3},{3,2},{4,5},{5,4},{6,7},{7,6},{8,9},{9,8},{10,11... | collective-permute-start | bytes 245768 | tf_op jit(solution)/shard_map/ppermute | solution.py:635
  12.1 11.1 %collective-permute-start.4 = (f32[38,8,128]{2,1,0:T(8,128)S(1)}, f32[38,8,128]{2,1,0:T(8,128)S(1)}, u32[]{:S(2)}, u32[]{:S(2)}) collective-permute-start(f32[38,8,128]{2,1,0:T(8,128)S(1)} %get-tuple-element.53), channel_id=1, source_target_pairs={{1,2},{2,1},{3,4},{4,3},{5,6},{6,5},{7,8},{8,7},{9,10},{10,9},{11,... | collective-permute-start | bytes 466952 | tf_op jit(solution)/shard_map/ppermute | solution.py:635
  15.2 8.0 %collective-permute-start.5 = (f32[38,8,128]{2,1,0:T(8,128)S(1)}, f32[38,8,128]{2,1,0:T(8,128)S(1)}, u32[]{:S(2)}, u32[]{:S(2)}) collective-permute-start(f32[38,8,128]{2,1,0:T(8,128)S(1)} %get-tuple-element.54), channel_id=1, source_target_pairs={{0,1},{1,0},{2,3},{3,2},{4,5},{5,4},{6,7},{7,6},{8,9},{9,8},{10,11... | collective-permute-start | bytes 466952 | tf_op jit(solution)/shard_map/ppermute | solution.py:635
  15.2 8.0 %collective-permute-start.2 = (f32[37,8,128]{2,1,0:T(8,128)S(1)}, f32[37,8,128]{2,1,0:T(8,128)S(1)}, u32[]{:S(2)}, u32[]{:S(2)}) collective-permute-start(f32[37,8,128]{2,1,0:T(8,128)S(1)} %get-tuple-element.51), channel_id=1, source_target_pairs={{16,32},{32,16},{48,64},{64,48},{80,96},{96,80},{112,128},{128,112... | collective-permute-start | bytes 454664 | tf_op jit(solution)/shard_map/ppermute | solution.py:635
  18.8 4.4 %collective-permute-start.3 = (f32[37,8,128]{2,1,0:T(8,128)S(1)}, f32[37,8,128]{2,1,0:T(8,128)S(1)}, u32[]{:S(2)}, u32[]{:S(2)}) collective-permute-start(f32[37,8,128]{2,1,0:T(8,128)S(1)} %get-tuple-element.52), channel_id=1, source_target_pairs={{0,16},{16,0},{32,48},{48,32},{64,80},{80,64},{96,112},{112,96},{1... | collective-permute-start | bytes 454664 | tf_op jit(solution)/shard_map/ppermute | solution.py:635
  23.7 8.4 %collective-permute-start.6 = (f32[41,8,128]{2,1,0:T(8,128)S(1)}, f32[41,8,128]{2,1,0:T(8,128)S(1)}, u32[]{:S(2)}, u32[]{:S(2)}) collective-permute-start(f32[41,8,128]{2,1,0:T(8,128)S(1)} %get-tuple-element.57.payload), channel_id=1, source_target_pairs={{1,2},{2,1},{3,4},{4,3},{5,6},{6,5},{7,8},{8,7},{9,10},{10,9},{11,... | collective-permute-start | bytes 503816 | tf_op jit(solution)/shard_map/ppermute | solution.py:635
  25.3 6.9 %collective-permute-start.7 = (f32[41,8,128]{2,1,0:T(8,128)S(1)}, f32[41,8,128]{2,1,0:T(8,128)S(1)}, u32[]{:S(2)}, u32[]{:S(2)}) collective-permute-start(f32[41,8,128]{2,1,0:T(8,128)S(1)} %get-tuple-element.57.payload), channel_id=1, source_target_pairs={{0,1},{1,0},{2,3},{3,2},{4,5},{5,4},{6,7},{7,6},{8,9},{9,8},{10,11... | collective-permute-start | bytes 503816 | tf_op jit(solution)/shard_map/ppermute | solution.py:635
